TPU v7x, 32 devices: a whole 2x2x4 slice. The times are simulated.
32 devices in a mesh: groups: 2 (over y), seq: 4 (over z), head: 4 (over x, core).
Axes of the slice: x: 2, y: 2, z: 4, core: 2. Of those that a mesh axis runs over, the one named last changes fastest.
Arguments:
- doc_start: int32 [1024], P(('groups', 'seq')), parts along dimension 0, may hold values from 0 to 511, as said below
- q_gdn: bfloat16 [1024, 2048], P(('groups', 'seq'), 'head'), parts along dimension 0, may hold values from -6 to 6
- k_gdn: bfloat16 [1024, 2048], P(('groups', 'seq'), 'head'), parts along dimension 0, may hold values from -6 to 6
- v_gdn: bfloat16 [1024, 4096], P(('groups', 'seq'), 'head'), parts along dimension 0, may hold values from -6 to 6
- z_gdn: bfloat16 [1024, 4096], P(('groups', 'seq'), 'head'), parts along dimension 0, may hold values from -6 to 6
- beta_logit: float32 [32, 1024], P('head', ('groups', 'seq')), parts along dimension 1, may hold values from -8 to 3
- log_decay: float32 [32, 1024], P('head', ('groups', 'seq')), parts along dimension 1, may hold values from -1 to 0
- norm_weight: float32 [128], replicated, may hold values from 0.1 to 1.9
- q_attn: bfloat16 [1024, 4096], P(('groups', 'seq'), 'head'), parts along dimension 0, may hold values from -6 to 6
- k_attn: bfloat16 [1024, 512], P(('groups', 'seq')), parts along dimension 0, may hold values from -6 to 6
- v_attn: bfloat16 [1024, 512], P(('groups', 'seq')), parts along dimension 0, may hold values from -6 to 6
- gate_attn: bfloat16 [1024, 4096], P(('groups', 'seq'), 'head'), parts along dimension 0, may hold values from -6 to 6
Outputs:
- gdn_out: bfloat16 [1024, 4096], P(('groups', 'seq'), 'head'), parts along dimension 0
- attn_out: bfloat16 [1024, 4096], P(('groups', 'seq'), 'head'), parts along dimension 0
There are 2 independent parts, one for each index of `groups`. A program takes and returns all parts, laid end to end along the dimension named above; an argument that names none is the same for every part. Nothing has to cross between parts.
Inputs may be any that keep to these rules, and one draw needn't show every extreme that they name: Nondecreasing; doc_start[i] <= i, with equality exactly at the first token of each of the 3 documents; the first document starts at 0.
All inputs are finite; a program needn't handle non-finite values.
Results may differ from a plain program's by a relative error of at most 0.0095.
Values may be sent and summed in bfloat16 or wider, within the bound.
A program may use at most 128 MiB of HBM per device.

v0:
```python
import jax
import jax.numpy as jnp
from jax import lax
from jax.sharding import PartitionSpec as P

DK = 128
DV = 128
QH = 16
KVH = 2
HD_A = 256
BLOCK = 64
HIGH = lax.Precision.HIGHEST


def shifted(shard, axis, by):
    length = lax.axis_size(axis)
    pairs = [(i, i + by) for i in range(length) if 0 <= i + by < length]
    return lax.ppermute(shard, axis, pairs)


def unit_rows(values):
    return values * lax.rsqrt(jnp.sum(values * values, axis=-1, keepdims=True) + 1e-06)


def blocked(values, count):
    length, heads, width = values.shape
    return values.reshape(count, length // count, heads, width).transpose(0, 2, 1, 3)


def block_terms(anchor, doc_block, query, keys, values, beta, log_gate):
    width = query.shape[1]
    running = jnp.cumsum(log_gate, axis=1)
    place = anchor + jnp.arange(width, dtype=jnp.int32)
    causal = place[None, :] <= place[:, None]
    same = causal & (doc_block[:, None] <= place[None, :])
    strict = same & (place[None, :] < place[:, None])
    spread = jnp.where(same[None], running[:, :, None] - running[:, None, :], 0.0)
    decay = jnp.where(same[None], jnp.exp(spread), 0.0)
    alive = (doc_block < anchor).astype(jnp.float32)
    entry = jnp.exp(running) * alive[None, :]
    gram = jnp.einsum("hik,hjk->hij", keys, keys, precision=HIGH)
    lower_part = jnp.where(strict[None], decay * gram, 0.0)
    system = jnp.eye(width, dtype=jnp.float32)[None] + beta[:, :, None] * lower_part
    right = jnp.concatenate([beta[:, :, None] * values, (beta * entry)[:, :, None] * keys], axis=2)
    solved = lax.linalg.triangular_solve(
        system, right, left_side=True, lower=True, unit_diagonal=True
    )
    fresh = solved[:, :, : values.shape[2]]
    erased = solved[:, :, values.shape[2] :]
    scores = jnp.einsum("hik,hjk->hij", query, keys, precision=HIGH) * decay
    local_out = jnp.einsum("hij,hjv->hiv", scores, fresh, precision=HIGH)
    reach = entry[:, :, None] * query - jnp.einsum("hij,hjk->hik", scores, erased, precision=HIGH)
    tail_keys = decay[:, -1, :, None] * keys
    identity = jnp.eye(keys.shape[2], dtype=jnp.float32)
    carry_map = entry[:, -1, None, None] * identity[None] - jnp.einsum(
        "hjk,hjl->hkl", erased, tail_keys, precision=HIGH
    )
    carry_add = jnp.einsum("hjv,hjk->hvk", fresh, tail_keys, precision=HIGH)
    return (local_out, reach, carry_map, carry_add)


def compose(earlier, later):
    joined_map = jnp.einsum("hkl,hlm->hkm", earlier[0], later[0], precision=HIGH)
    joined_add = jnp.einsum("hvl,hlm->hvm", earlier[1], later[0], precision=HIGH) + later[1]
    return (joined_map, joined_add)


def entering_state(device_map, device_add):

    def relay(turn, pair):
        incoming, state = pair
        incoming = shifted(state.astype(jnp.bfloat16), "seq", 1).astype(state.dtype)
        state = jnp.einsum("hvk,hkl->hvl", incoming, device_map, precision=HIGH) + device_add
        return (incoming, state)

    start_state, _ = lax.fori_loop(
        0, lax.axis_size("seq") - 1, relay, (jnp.zeros_like(device_add), device_add)
    )
    return start_state


def delta_layer(doc_start, q_gdn, k_gdn, v_gdn, z_gdn, beta_logit, log_decay, norm_weight, anchor):
    length = q_gdn.shape[0]
    key_heads = q_gdn.shape[1] // DK
    value_heads = v_gdn.shape[1] // DV
    repeat = value_heads // key_heads
    count = length // BLOCK
    query = jnp.repeat(
        unit_rows(q_gdn.astype(jnp.float32).reshape(length, key_heads, DK)), repeat, axis=1
    )
    keys = jnp.repeat(
        unit_rows(k_gdn.astype(jnp.float32).reshape(length, key_heads, DK)), repeat, axis=1
    )
    values = v_gdn.astype(jnp.float32).reshape(length, value_heads, DV)
    beta = jax.nn.sigmoid(beta_logit).reshape(value_heads, count, BLOCK).transpose(1, 0, 2)
    log_gate = log_decay.reshape(value_heads, count, BLOCK).transpose(1, 0, 2)
    docs = doc_start.reshape(count, BLOCK)
    anchors = anchor + BLOCK * jnp.arange(count, dtype=jnp.int32)
    identity = jnp.broadcast_to(jnp.eye(DK, dtype=jnp.float32), (value_heads, DK, DK))

    def sweep(totals, inputs):
        total_map, total_add = totals
        block_anchor, doc_block, q_block, k_block, v_block, b_block, g_block = inputs
        local_out, reach, carry_map, carry_add = block_terms(
            block_anchor, doc_block, q_block, k_block, v_block, b_block, g_block
        )
        joined = compose((total_map, total_add), (carry_map, carry_add))
        return (joined, (local_out, reach, total_map, total_add))

    start_totals = (identity, jnp.zeros((value_heads, DV, DK), jnp.float32))
    scanned = (
        anchors,
        docs,
        blocked(query, count),
        blocked(keys, count),
        blocked(values, count),
        beta,
        log_gate,
    )
    (device_map, device_add), (local_out, reach, prefix_map, prefix_add) = lax.scan(
        sweep, start_totals, scanned
    )
    start_state = entering_state(device_map, device_add)
    block_state = jnp.einsum("hvk,chkl->chvl", start_state, prefix_map, precision=HIGH) + prefix_add
    mixed = local_out + jnp.einsum("chik,chvk->chiv", reach, block_state, precision=HIGH)
    mixed = mixed.transpose(0, 2, 1, 3).reshape(length, value_heads, DV)
    gate = z_gdn.astype(jnp.float32).reshape(length, value_heads, DV)
    factor = lax.rsqrt(jnp.mean(mixed * mixed, axis=-1, keepdims=True) + 1e-06)
    normed = mixed * factor * norm_weight * jax.nn.silu(gate)
    return normed.reshape(length, value_heads * DV).astype(jnp.bfloat16)


def attend(doc_start, q_attn, k_attn, v_attn, gate_attn, anchor):
    length = q_attn.shape[0]
    local_heads = q_attn.shape[1] // HD_A
    group = QH // KVH
    shards_seen = lax.axis_size("seq") // 2 + 1
    window_size = shards_seen * length
    kv_head = lax.axis_index("head") * local_heads // group
    keys_own = lax.dynamic_slice_in_dim(k_attn, kv_head * HD_A, HD_A, 1)
    values_own = lax.dynamic_slice_in_dim(v_attn, kv_head * HD_A, HD_A, 1)
    query = q_attn.reshape(length, local_heads, HD_A)
    q_place = anchor + jnp.arange(length, dtype=jnp.int32)
    lower = jnp.maximum(doc_start, q_place - window_size + 1)
    lowest = jnp.min(lower)
    highest = anchor + length - 1
    factor = HD_A ** (-0.5)
    initial = (
        jnp.full((local_heads, length), -1e30, jnp.float32),
        jnp.zeros((local_heads, length), jnp.float32),
        jnp.zeros((local_heads, length, HD_A), jnp.float32),
    )
    key_piece = lax.all_gather(keys_own, "seq", axis=0, tiled=True)
    value_piece = lax.all_gather(values_own, "seq", axis=0, tiled=True)
    count = key_piece.shape[0]
    width = count
    while width > 1024 and width % 2 == 0:
        width = width // 2

    def one(index, inner):
        begin = index * width
        key_part = lax.dynamic_slice_in_dim(key_piece, begin, width, 0)
        value_part = lax.dynamic_slice_in_dim(value_piece, begin, width, 0)
        k_place = begin + jnp.arange(width, dtype=jnp.int32)

        def compute(state):
            peak, total, accum = state
            scores = (
                jnp.einsum("qhd,kd->hqk", query, key_part, preferred_element_type=jnp.float32)
                * factor
            )
            visible = (k_place[None, :] >= lower[:, None]) & (k_place[None, :] <= q_place[:, None])
            masked = jnp.where(visible[None], scores, -jnp.inf)
            new_peak = jnp.maximum(peak, jnp.max(masked, axis=-1))
            weights = jnp.exp(masked - new_peak[:, :, None])
            shrink = jnp.exp(peak - new_peak)
            total = total * shrink + jnp.sum(weights, axis=-1)
            update = jnp.einsum(
                "hqk,kd->hqd",
                weights.astype(jnp.bfloat16),
                value_part,
                preferred_element_type=jnp.float32,
            )
            accum = accum * shrink[:, :, None] + update
            return (new_peak, total, accum)

        def unchanged(state):
            return state

        busy = (begin <= highest) & (begin + width - 1 >= lowest)
        return lax.cond(busy, compute, unchanged, inner)

    peak, total, accum = lax.fori_loop(0, count // width, one, initial)
    mixed = (accum / total[:, :, None]).transpose(1, 0, 2).reshape(length, local_heads * HD_A)
    return (mixed * jax.nn.sigmoid(gate_attn.astype(jnp.float32))).astype(jnp.bfloat16)


def shards(
    doc_start,
    q_gdn,
    k_gdn,
    v_gdn,
    z_gdn,
    beta_logit,
    log_decay,
    norm_weight,
    q_attn,
    k_attn,
    v_attn,
    gate_attn,
):
    anchor = lax.axis_index("seq") * q_gdn.shape[0]
    gdn_out = delta_layer(
        doc_start, q_gdn, k_gdn, v_gdn, z_gdn, beta_logit, log_decay, norm_weight, anchor
    )
    attn_out = attend(doc_start, q_attn, k_attn, v_attn, gate_attn, anchor)
    return (gdn_out, attn_out)


def solution(mesh):
    return jax.shard_map(
        shards,
        mesh=mesh,
        in_specs=(
            P(("groups", "seq")),
            P(("groups", "seq"), "head"),
            P(("groups", "seq"), "head"),
            P(("groups", "seq"), "head"),
            P(("groups", "seq"), "head"),
            P("head", ("groups", "seq")),
            P("head", ("groups", "seq")),
            P(),
            P(("groups", "seq"), "head"),
            P(("groups", "seq"), None),
            P(("groups", "seq"), None),
            P(("groups", "seq"), "head"),
        ),
        out_specs=(P(("groups", "seq"), "head"), P(("groups", "seq"), "head")),
        check_vma=False,
    )
```

profile of v0, /device:TPU:0, one launch (start us, length us, event | category | flops | bytes accessed | tf_op | source)
XLA Modules:
  0.0 189.3 jit_solution(7092509554987152704)
XLA Ops:
  0.7 1.0 reshape.347
  2.2 0.9 copy-done.16
  3.7 0.9 copy-done.13
  4.7 0.8 bitcast_bitcast_fusion
  5.7 0.6 copy-done.19
  7.1 0.7 copy-done.21
  7.8 105.6 %while.13 = (s32[]{:T(128)}, f32[8,128,128]{1,2,0:T(8,128)S(1)}, f32[8,128,128]{1,2,0:T(8,128)S(1)}, f32[2,8,64,128]{3,2,1,0:T(8,128)}, f32[2,8,64,128]{3,2,1,0:...) while((s32[]{:T(128)}, f32[8,128,128]{1,2,0:T(8,128)S(1)}, ...), condition=%wide.region_4.5_spmd.clone, body=%wide.region_2.4_spmd.clone.sunk | while | flops 907780864 | bytes 40192524 | solution.py:120
  8.4 0.6 iota_add_fusion.5
  10.1 39.3 %custom-call.11 = f32[8,1,64,64]{2,3,1,0:T(8,128)S(1)} custom-call(f32[8,1,64,64]{3,2,1,0:T(8,128)S(1)} %fusion.124), custom_call_target="InvertDiagBlocksLowerTriangular" | custom-call | tf_op jit(solution)/shard_map/while/body/eval_jaxpr/triangular_solve | solution.py:45
  49.4 0.7 fusion.120
  50.3 1.0 constant_dynamic-slice_fusion.9
  51.4 0.6 fusion.125
  52.4 1.1 convolution_subtract_fusion.3
  53.5 1.0 convolution_bitcast_fusion.7
  55.2 1.1 convolution_add_fusion.7
  56.3 1.0 convolution_bitcast_fusion.6
  59.8 0.8 copy-done.8
  61.2 0.6 iota_add_fusion.5
  62.9 39.3 %custom-call.11 = f32[8,1,64,64]{2,3,1,0:T(8,128)S(1)} custom-call(f32[8,1,64,64]{3,2,1,0:T(8,128)S(1)} %fusion.124), custom_call_target="InvertDiagBlocksLowerTriangular" | custom-call | tf_op jit(solution)/shard_map/while/body/eval_jaxpr/triangular_solve | solution.py:45
  102.2 0.7 fusion.120
  103.1 1.0 constant_dynamic-slice_fusion.9
  105.2 1.1 convolution_subtract_fusion.3
  106.3 1.0 convolution_bitcast_fusion.7
  108.0 1.1 convolution_add_fusion.7
  109.1 1.0 convolution_bitcast_fusion.6
  112.7 0.8 copy-done.8
  113.6 0.7 convert.19
  114.6 34.6 %while.12 = (s32[]{:T(128)}, f32[8,128,128]{2,1,0:T(8,128)}, bf16[8,128,128]{2,1,0:T(8,128)(2,1)}, f32[8,128,128]{2,1,0:T(8,128)S(1)}, f32[8,128,128]{2,1,0:T(8,128)S(1)}, /*index=5*/s32[]{:T(128)}) while((s32[]{:T(128)}, f32[8,128,128]{2,1,0:T(8,128)}, bf16[8,128,128]{2,1,0:T(8,128)(2,1)}, f32[8,128,128]{2,1,0:T(8,128)S(1)}, ...), condition=%wide.region_6.7_spmd, body=%wide.region_5.6_spmd.sunk | while | flops 201719808 | bytes 3407981 | solution.py:76
  114.6 5.1 %collective-permute-start = (bf16[8,128,128]{2,1,0:T(8,128)(2,1)}, bf16[8,128,128]{2,1,0:T(8,128)(2,1)S(1)}, u32[]{:S(2)}, u32[]{:S(2)}) collective-permute-start(bf16[8,128,128]{2,1,0:T(8,128)(2,1)} %get-tuple-element.581), channel_id=1, source_target_pairs={{0,4},{4,8},{8,12},{1,5},{5,9},{9,13},{2,6},{6,10},{10,14},{3,7},{... | collective-permute-start | bytes 786440 | tf_op jit(solution)/shard_map/while/body/eval_jaxpr/ppermute | solution.py:18
  119.8 5.8 %collective-permute-done = bf16[8,128,128]{2,1,0:T(8,128)(2,1)S(1)} collective-permute-done((bf16[8,128,128]{2,1,0:T(8,128)(2,1)}, bf16[8,128,128]{2,1,0:T(8,128)(2,1)S(1)}, u32[]{:S(2)}, u32[]{:S(2)}) %collective-permute-start) | collective-permute-done | bytes 262176 | tf_op jit(solution)/shard_map/while/body/eval_jaxpr/ppermute | solution.py:18
  125.6 0.8 convert_element_type.81
  126.4 1.1 convolution_add_fusion.6
  127.5 4.3 %collective-permute-start = (bf16[8,128,128]{2,1,0:T(8,128)(2,1)}, bf16[8,128,128]{2,1,0:T(8,128)(2,1)S(1)}, u32[]{:S(2)}, u32[]{:S(2)}) collective-permute-start(bf16[8,128,128]{2,1,0:T(8,128)(2,1)} %get-tuple-element.581), channel_id=1, source_target_pairs={{0,4},{4,8},{8,12},{1,5},{5,9},{9,13},{2,6},{6,10},{10,14},{3,7},{... | collective-permute-start | bytes 786440 | tf_op jit(solution)/shard_map/while/body/eval_jaxpr/ppermute | solution.py:18
  131.8 5.0 %collective-permute-done = bf16[8,128,128]{2,1,0:T(8,128)(2,1)S(1)} collective-permute-done((bf16[8,128,128]{2,1,0:T(8,128)(2,1)}, bf16[8,128,128]{2,1,0:T(8,128)(2,1)S(1)}, u32[]{:S(2)}, u32[]{:S(2)}) %collective-permute-start) | collective-permute-done | bytes 262176 | tf_op jit(solution)/shard_map/while/body/eval_jaxpr/ppermute | solution.py:18
  136.8 0.8 convert_element_type.81
  137.7 1.1 convolution_add_fusion.6
  138.8 4.3 %collective-permute-start = (bf16[8,128,128]{2,1,0:T(8,128)(2,1)}, bf16[8,128,128]{2,1,0:T(8,128)(2,1)S(1)}, u32[]{:S(2)}, u32[]{:S(2)}) collective-permute-start(bf16[8,128,128]{2,1,0:T(8,128)(2,1)} %get-tuple-element.581), channel_id=1, source_target_pairs={{0,4},{4,8},{8,12},{1,5},{5,9},{9,13},{2,6},{6,10},{10,14},{3,7},{... | collective-permute-start | bytes 786440 | tf_op jit(solution)/shard_map/while/body/eval_jaxpr/ppermute | solution.py:18
  143.1 4.2 %collective-permute-done = bf16[8,128,128]{2,1,0:T(8,128)(2,1)S(1)} collective-permute-done((bf16[8,128,128]{2,1,0:T(8,128)(2,1)}, bf16[8,128,128]{2,1,0:T(8,128)(2,1)S(1)}, u32[]{:S(2)}, u32[]{:S(2)}) %collective-permute-start) | collective-permute-done | bytes 262176 | tf_op jit(solution)/shard_map/while/body/eval_jaxpr/ppermute | solution.py:18
  147.2 0.8 convert_element_type.81
  148.1 1.1 convolution_add_fusion.6
  149.2 2.2 %fusion.53 = f32[2,8,128,128]{2,3,1,0:T(8,128)S(1)} fusion(f32[2,8,128,128]{2,3,1,0:T(8,128)S(1)} %copy-done.6, f32[2,8,128,128]{2,3,1,0:T(8,128)S(1)} %copy-done.3, f32[8,128,128]{2,1,0:T(8,128)} %get-tuple-element.215), kind=kOutput, calls=%fused_computation.91 | convolution fusion | flops 402915328 | bytes 3670016 | tf_op jit(solution)/shard_map/hvk,chkl->chvl/dot_general | solution.py:124
  151.4 1.1 multiply_reduce_fusion
  153.9 1.0 fusion.61
  154.9 15.6 %all_gather.6 = bf16[512,256]{1,0:T(8,128)(2,1)S(1)} all-gather(bf16[128,256]{1,0:T(8,128)(2,1)S(1)} %constant_dynamic-slice_fusion.5), channel_id=1, replica_groups=mesh['groups'=2,'seq'=4,'head'=4] {'seq'}, dimensions={0}, use_global_device_ids=true | all-gather | bytes 327680 | tf_op jit(solution)/shard_map/all_gather | solution.py:153
  170.5 14.0 %all_gather.7 = bf16[512,256]{1,0:T(8,128)(2,1)S(1)} all-gather(bf16[128,256]{1,0:T(8,128)(2,1)S(1)} %constant_dynamic-slice_fusion.4), channel_id=1, replica_groups=mesh['groups'=2,'seq'=4,'head'=4] {'seq'}, dimensions={0}, use_global_device_ids=true | all-gather | bytes 327680 | tf_op jit(solution)/shard_map/all_gather | solution.py:154
  186.1 1.2 conditional.1
  187.6 0.9 copy-done.15
  188.5 0.8 multiply_convert_fusion
  (143 shorter events, 17.2 us)
Async XLA Ops:
  0.6 154.2 %copy-start = (bf16[128,512]{1,0:T(8,128)(2,1)S(1)}, bf16[128,512]{1,0:T(8,128)(2,1)}, u32[]{:S(2)}) copy-start(bf16[128,512]{1,0:T(8,128)(2,1)} %param.27) | copy-start | bytes 393220
  2.2 0.9 copy-start.16
  3.6 1.0 copy-start.13
  5.6 0.7 copy-start.19
  6.3 0.7 copy-start.18
  7.1 0.7 copy-start.21
  53.5 1.2 copy-start.1
  53.5 1.5 copy-start.4
  55.1 2.2 %copy-start.2 = (f32[2,8,128,128]{2,3,1,0:T(8,128)}, f32[2,8,128,128]{2,3,1,0:T(8,128)S(1)}, u32[]{:S(2)}) copy-start(f32[2,8,128,128]{2,3,1,0:T(8,128)S(1)} %get-tuple-element.561) | copy-start | bytes 3145732 | tf_op jit(solution)/shard_map/while
  55.2 2.2 %copy-start.5 = (f32[2,8,128,128]{2,3,1,0:T(8,128)}, f32[2,8,128,128]{2,3,1,0:T(8,128)S(1)}, u32[]{:S(2)}) copy-start(f32[2,8,128,128]{2,3,1,0:T(8,128)S(1)} %get-tuple-element.562) | copy-start | bytes 3145732 | tf_op jit(solution)/shard_map/while
  57.3 1.0 copy-start.10
  58.4 1.0 copy-start.7
  58.8 1.0 copy-start.11
  59.8 0.8 copy-start.8
  106.3 1.2 copy-start.1
  106.3 1.5 copy-start.4
  108.0 2.2 %copy-start.2 = (f32[2,8,128,128]{2,3,1,0:T(8,128)}, f32[2,8,128,128]{2,3,1,0:T(8,128)S(1)}, u32[]{:S(2)}) copy-start(f32[2,8,128,128]{2,3,1,0:T(8,128)S(1)} %get-tuple-element.561) | copy-start | bytes 3145732 | tf_op jit(solution)/shard_map/while
  108.0 2.2 %copy-start.5 = (f32[2,8,128,128]{2,3,1,0:T(8,128)}, f32[2,8,128,128]{2,3,1,0:T(8,128)S(1)}, u32[]{:S(2)}) copy-start(f32[2,8,128,128]{2,3,1,0:T(8,128)S(1)} %get-tuple-element.562) | copy-start | bytes 3145732 | tf_op jit(solution)/shard_map/while
  110.2 1.0 copy-start.10
  111.2 1.0 copy-start.7
  111.6 1.0 copy-start.11
  112.6 0.8 copy-start.8
  114.6 34.6 %copy-start.3 = (f32[2,8,128,128]{2,3,1,0:T(8,128)S(1)}, f32[2,8,128,128]{2,3,1,0:T(8,128)}, u32[]{:S(2)}) copy-start(f32[2,8,128,128]{2,3,1,0:T(8,128)} %get-tuple-element.212) | copy-start | bytes 3145732
  114.6 34.6 %copy-start.6 = (f32[2,8,128,128]{2,3,1,0:T(8,128)S(1)}, f32[2,8,128,128]{2,3,1,0:T(8,128)}, u32[]{:S(2)}) copy-start(f32[2,8,128,128]{2,3,1,0:T(8,128)} %get-tuple-element.216) | copy-start | bytes 3145732
  114.6 11.0 %collective-permute-start = (bf16[8,128,128]{2,1,0:T(8,128)(2,1)}, bf16[8,128,128]{2,1,0:T(8,128)(2,1)S(1)}, u32[]{:S(2)}, u32[]{:S(2)}) collective-permute-start(bf16[8,128,128]{2,1,0:T(8,128)(2,1)} %get-tuple-element.581), channel_id=1, source_target_pairs={{0,4},{4,8},{8,12},{1,5},{5,9},{9,13},{2,6},{6,10},{10,14},{3,7},{... | collective-permute-start | bytes 786440 | tf_op jit(solution)/shard_map/while/body/eval_jaxpr/ppermute | solution.py:18
  127.5 9.3 %collective-permute-start = (bf16[8,128,128]{2,1,0:T(8,128)(2,1)}, bf16[8,128,128]{2,1,0:T(8,128)(2,1)S(1)}, u32[]{:S(2)}, u32[]{:S(2)}) collective-permute-start(bf16[8,128,128]{2,1,0:T(8,128)(2,1)} %get-tuple-element.581), channel_id=1, source_target_pairs={{0,4},{4,8},{8,12},{1,5},{5,9},{9,13},{2,6},{6,10},{10,14},{3,7},{... | collective-permute-start | bytes 786440 | tf_op jit(solution)/shard_map/while/body/eval_jaxpr/ppermute | solution.py:18
  138.8 8.5 %collective-permute-start = (bf16[8,128,128]{2,1,0:T(8,128)(2,1)}, bf16[8,128,128]{2,1,0:T(8,128)(2,1)S(1)}, u32[]{:S(2)}, u32[]{:S(2)}) collective-permute-start(bf16[8,128,128]{2,1,0:T(8,128)(2,1)} %get-tuple-element.581), channel_id=1, source_target_pairs={{0,4},{4,8},{8,12},{1,5},{5,9},{9,13},{2,6},{6,10},{10,14},{3,7},{... | collective-permute-start | bytes 786440 | tf_op jit(solution)/shard_map/while/body/eval_jaxpr/ppermute | solution.py:18
  149.2 2.2 %copy-start.9 = (f32[2,8,64,128]{3,2,1,0:T(8,128)S(1)}, f32[2,8,64,128]{3,2,1,0:T(8,128)}, u32[]{:S(2)}) copy-start(f32[2,8,64,128]{3,2,1,0:T(8,128)} %get-tuple-element.210) | copy-start | bytes 1572868
  149.2 2.2 %copy-start.12 = (f32[2,8,64,128]{3,2,1,0:T(8,128)S(1)}, f32[2,8,64,128]{3,2,1,0:T(8,128)}, u32[]{:S(2)}) copy-start(f32[2,8,64,128]{3,2,1,0:T(8,128)} %get-tuple-element.211) | copy-start | bytes 1572868
  152.9 1.0 copy-start.14
  153.2 0.7 copy-start.20
  154.9 15.6 %copy-start.17 = (bf16[128,512]{1,0:T(8,128)(2,1)S(1)}, bf16[128,512]{1,0:T(8,128)(2,1)}, u32[]{:S(2)}) copy-start(bf16[128,512]{1,0:T(8,128)(2,1)} %param.28) | copy-start | bytes 393220
  185.2 0.9 copy-start.22
  187.5 1.0 copy-start.15
where the time goes:
time: 190 us; the launch traced here: 189 us
  other arithmetic  90.3 us (48%)
  blocking collectives  29.7 us (16%)
  matrix products  21.1 us (11%)
  local copies, waits for them, and re-layouts  17.3 us (9%)
  waiting for transfers between devices  15 us (8%)
  starting transfers between devices  13.7 us (7%)
    another operation x6, other arithmetic, block_terms(): lax.linalg.triangular_solve(system, right, left_side=True, lower=True, un...  78.8 us
    all_gather x1, blocking collectives, attend(): key_piece = lax.all_gather(keys_own, 'seq', axis=0, tiled=True)  15.6 us
    ppermute x3, waiting for transfers between devices, shifted(): return lax.ppermute(shard, axis, pairs)  15 us
    all_gather x1, blocking collectives, attend(): value_piece = lax.all_gather(values_own, 'seq', axis=0, tiled=True)  14 us
    ppermute x3, starting transfers between devices, shifted(): return lax.ppermute(shard, axis, pairs)  13.7 us
    unnamed x31, local copies, waits for them, and re-layouts  5.57 us
    while x34, local copies, waits for them, and re-layouts  4.8 us
  transfers between devices with their start and end apart: 3, of which 3 were waited for; matrix products, arithmetic and copies ran while one was open for 0% of the time, Pallas kernels for 0%

commit v1 on v0

--- a/solution.py
+++ b/solution.py
@@ -10,6 +10,27 @@
 HD_A = 256
 BLOCK = 64
 HIGH = lax.Precision.HIGHEST
+
+
+def ring_gather(x, axis, dim):
+    peers, position, width = (lax.axis_size(axis), lax.axis_index(axis), x.shape[dim])
+    right = [(i, (i + 1) % peers) for i in range(peers)]
+    left = [(i, (i - 1) % peers) for i in range(peers)]
+    out = jnp.zeros((*x.shape[:dim], peers * width, *x.shape[dim + 1 :]), x.dtype)
+    out = lax.dynamic_update_slice_in_dim(out, x, position * width, axis=dim)
+    from_left = from_right = x
+    half = peers // 2
+    for step in range(1, half + 1):
+        from_left = lax.ppermute(from_left, axis, right)
+        out = lax.dynamic_update_slice_in_dim(
+            out, from_left, (position - step) % peers * width, axis=dim
+        )
+        if step < peers - half:
+            from_right = lax.ppermute(from_right, axis, left)
+            out = lax.dynamic_update_slice_in_dim(
+                out, from_right, (position + step) % peers * width, axis=dim
+            )
+    return out
 
 
 def shifted(shard, axis, by):
@@ -150,7 +171,7 @@
         jnp.zeros((local_heads, length), jnp.float32),
         jnp.zeros((local_heads, length, HD_A), jnp.float32),
     )
-    key_piece = lax.all_gather(keys_own, "seq", axis=0, tiled=True)
+    key_piece = ring_gather(keys_own, "seq", 0)
     value_piece = lax.all_gather(values_own, "seq", axis=0, tiled=True)
     count = key_piece.shape[0]
     width = count

time: 190 us -> 186 us (0.979)
  blocking collectives: 29.7 us -> 14.1 us
  starting transfers between devices: 13.7 us -> 18.5 us
  local copies, waits for them, and re-layouts: 17.3 us -> 21.1 us
  matrix products: 21.1 us -> 24.7 us
  waiting for transfers between devices: 15 us -> 12.9 us
    all_gather x1 -> x0, blocking collectives: 15.6 us -> none  [attend(): key_piece = lax.all_gather(keys_own, 'seq', axis=0, tiled=True)]
    ppermute x0 -> x3, starting transfers between devices: none -> 7.61 us  [the longest x2 5.59 us: ring_gather(): from_left = lax.ppermute(from_left, axis, right)]
    dynamic_update_slice x0 -> x4, local copies, waits for them, and re-layouts: none -> 4.44 us  [the longest x2 1.83 us: ring_gather(): lax.dynamic_update_slice_in_dim(out, from_left, (position - step) % peers...]
    ppermute x3, starting transfers between devices: 13.7 us -> 10.9 us  [shifted(): return lax.ppermute(shard, axis, pairs)]
    dot_general x3, matrix products: 3.32 us -> 1.2 us  [relay(): jnp.einsum('hvk,hkl->hvl', incoming, device_map, precision=HIGH)]
    ppermute x3, waiting for transfers between devices: 15 us -> 12.9 us  [shifted(): return lax.ppermute(shard, axis, pairs)]
    while x34 -> x50, local copies, waits for them, and re-layouts: 4.8 us -> 3.34 us
  transfers between devices with their start and end apart: 3 -> 6, of which waited for: 3 -> 3; matrix products, arithmetic and copies ran while one was open for 0% -> 65% of each run, Pallas kernels for 0% -> 0%
where the time goes in v1:
time: 186 us; the launch traced here: 185 us
  other arithmetic  91.5 us (49%)
  matrix products  24.7 us (13%)
  local copies, waits for them, and re-layouts  21.1 us (11%)
  starting transfers between devices  18.5 us (10%)
  blocking collectives  14.1 us (8%)
  waiting for transfers between devices  12.9 us (7%)
    another operation x6, other arithmetic, block_terms(): lax.linalg.triangular_solve(system, right, left_side=True, lower=True, un...  80.3 us
    all_gather x1, blocking collectives, attend(): value_piece = lax.all_gather(values_own, 'seq', axis=0, tiled=True)  14.1 us
    ppermute x3, waiting for transfers between devices, shifted(): return lax.ppermute(shard, axis, pairs)  12.9 us
    ppermute x3, starting transfers between devices, shifted(): return lax.ppermute(shard, axis, pairs)  10.9 us
    unnamed x31, local copies, waits for them, and re-layouts  7.29 us
    ppermute x2, starting transfers between devices, ring_gather(): from_left = lax.ppermute(from_left, axis, right)  5.59 us
  transfers between devices with their start and end apart: 6, of which 3 were waited for; matrix products, arithmetic and copies ran while one was open for 65% of the time, Pallas kernels for 0%

profile of v1, /device:TPU:0, one launch (start us, length us, event | category | flops | bytes accessed | tf_op | source)
XLA Modules:
  0.0 185.2 jit_solution(10616960518645199346)
XLA Ops:
  0.7 0.9 copy-done
  2.2 3.1 %collective-permute-start.1 = (bf16[128,256]{1,0:T(8,128)(2,1)}, bf16[128,256]{1,0:T(8,128)(2,1)}, u32[]{:S(2)}, u32[]{:S(2)}) collective-permute-start(bf16[128,256]{1,0:T(8,128)(2,1)} %constant_dynamic-slice_fusion.5), channel_id=1, source_target_pairs={{0,4},{4,8},{8,12},{12,0},{1,5},{5,9},{9,13},{13,1},{2,6},{6,10},{... | collective-permute-start | bytes 196616 | tf_op jit(solution)/shard_map/ppermute | solution.py:24
  5.2 2.0 %collective-permute-start.2 = (bf16[128,256]{1,0:T(8,128)(2,1)}, bf16[128,256]{1,0:T(8,128)(2,1)}, u32[]{:S(2)}, u32[]{:S(2)}) collective-permute-start(bf16[128,256]{1,0:T(8,128)(2,1)} %constant_dynamic-slice_fusion.5), channel_id=1, source_target_pairs={{0,12},{4,0},{8,4},{12,8},{1,13},{5,1},{9,5},{13,9},{2,14},{6,2},{... | collective-permute-start | bytes 196616 | tf_op jit(solution)/shard_map/ppermute | solution.py:29
  8.0 1.3 fusion.64
  9.9 0.9 copy-done.12
  11.4 0.9 copy-done.8
  14.6 109.3 %while.13 = (s32[]{:T(128)}, f32[8,128,128]{1,2,0:T(8,128)S(1)}, f32[8,128,128]{1,2,0:T(8,128)S(1)}, f32[2,8,64,128]{3,2,1,0:T(8,128)}, f32[2,8,64,128]{3,2,1,0:...) while((s32[]{:T(128)}, f32[8,128,128]{1,2,0:T(8,128)S(1)}, ...), condition=%wide.region_4.5_spmd.clone, body=%wide.region_2.4_spmd.clone.sunk | while | flops 907780864 | bytes 36036276 | solution.py:141
  16.5 0.7 constant_dynamic-slice_fusion.8
  17.5 1.3 fusion.124
  18.8 40.0 %custom-call.11 = f32[8,1,64,64]{2,3,1,0:T(8,128)S(1)} custom-call(f32[8,1,64,64]{3,2,1,0:T(8,128)} %fusion.124), custom_call_target="InvertDiagBlocksLowerTriangular" | custom-call | tf_op jit(solution)/shard_map/while/body/eval_jaxpr/triangular_solve | solution.py:66
  60.9 1.1 convolution_subtract_fusion.3
  62.0 1.0 convolution_bitcast_fusion.7
  63.7 1.1 convolution_add_fusion.7
  64.8 1.0 convolution_bitcast_fusion.6
  66.4 1.1 fusion.127
  67.5 1.1 fusion.126
  68.6 0.7 copy-done.14
  71.1 0.7 constant_dynamic-slice_fusion.8
  72.1 1.3 fusion.124
  73.4 40.0 %custom-call.11 = f32[8,1,64,64]{2,3,1,0:T(8,128)S(1)} custom-call(f32[8,1,64,64]{3,2,1,0:T(8,128)} %fusion.124), custom_call_target="InvertDiagBlocksLowerTriangular" | custom-call | tf_op jit(solution)/shard_map/while/body/eval_jaxpr/triangular_solve | solution.py:66
  115.5 1.1 convolution_subtract_fusion.3
  116.6 1.0 convolution_bitcast_fusion.7
  118.3 1.1 convolution_add_fusion.7
  119.4 1.0 convolution_bitcast_fusion.6
  121.0 1.1 fusion.127
  122.1 1.1 fusion.126
  124.3 27.6 %while.12 = (s32[]{:T(128)}, f32[8,128,128]{2,1,0:T(8,128)}, bf16[8,128,128]{2,1,0:T(8,128)(2,1)S(1)}, f32[8,128,128]{2,1,0:T(8,128)S(1)}, f32[8,128,128]{2,1,0:T(8,128)S(1)}, /*index=5*/s32[]{:T(128)}) while((s32[]{:T(128)}, f32[8,128,128]{2,1,0:T(8,128)}, bf16[8,128,128]{2,1,0:T(8,128)(2,1)S(1)}, f32[8,128,128]{2,1,0:T(8,128)S(1)}, ...), condition=%wide.region_6.7_spmd, body=%wide.region_5.6_spmd.sunk | while | flops 201719808 | bytes 3407981 | solution.py:97
  124.4 2.1 %collective-permute-start = (bf16[8,128,128]{2,1,0:T(8,128)(2,1)S(1)}, bf16[8,128,128]{2,1,0:T(8,128)(2,1)S(1)}, u32[]{:S(2)}, u32[]{:S(2)}) collective-permute-start(bf16[8,128,128]{2,1,0:T(8,128)(2,1)S(1)} %get-tuple-element.850), channel_id=1, source_target_pairs={{0,4},{4,8},{8,12},{1,5},{5,9},{9,13},{2,6},{6,10},{10,14},{3,7},{... | collective-permute-start | bytes 786440 | tf_op jit(solution)/shard_map/while/body/eval_jaxpr/ppermute | solution.py:39
  126.4 5.0 %collective-permute-done = bf16[8,128,128]{2,1,0:T(8,128)(2,1)S(1)} collective-permute-done((bf16[8,128,128]{2,1,0:T(8,128)(2,1)S(1)}, bf16[8,128,128]{2,1,0:T(8,128)(2,1)S(1)}, u32[]{:S(2)}, u32[]{:S(2)}) %collective-permute-start) | collective-permute-done | bytes 262176 | tf_op jit(solution)/shard_map/while/body/eval_jaxpr/ppermute | solution.py:39
  131.4 0.8 convert_element_type.83
  132.6 4.4 %collective-permute-start = (bf16[8,128,128]{2,1,0:T(8,128)(2,1)S(1)}, bf16[8,128,128]{2,1,0:T(8,128)(2,1)S(1)}, u32[]{:S(2)}, u32[]{:S(2)}) collective-permute-start(bf16[8,128,128]{2,1,0:T(8,128)(2,1)S(1)} %get-tuple-element.850), channel_id=1, source_target_pairs={{0,4},{4,8},{8,12},{1,5},{5,9},{9,13},{2,6},{6,10},{10,14},{3,7},{... | collective-permute-start | bytes 786440 | tf_op jit(solution)/shard_map/while/body/eval_jaxpr/ppermute | solution.py:39
  137.1 4.1 %collective-permute-done = bf16[8,128,128]{2,1,0:T(8,128)(2,1)S(1)} collective-permute-done((bf16[8,128,128]{2,1,0:T(8,128)(2,1)S(1)}, bf16[8,128,128]{2,1,0:T(8,128)(2,1)S(1)}, u32[]{:S(2)}, u32[]{:S(2)}) %collective-permute-start) | collective-permute-done | bytes 262176 | tf_op jit(solution)/shard_map/while/body/eval_jaxpr/ppermute | solution.py:39
  141.2 0.8 convert_element_type.83
  142.4 4.4 %collective-permute-start = (bf16[8,128,128]{2,1,0:T(8,128)(2,1)S(1)}, bf16[8,128,128]{2,1,0:T(8,128)(2,1)S(1)}, u32[]{:S(2)}, u32[]{:S(2)}) collective-permute-start(bf16[8,128,128]{2,1,0:T(8,128)(2,1)S(1)} %get-tuple-element.850), channel_id=1, source_target_pairs={{0,4},{4,8},{8,12},{1,5},{5,9},{9,13},{2,6},{6,10},{10,14},{3,7},{... | collective-permute-start | bytes 786440 | tf_op jit(solution)/shard_map/while/body/eval_jaxpr/ppermute | solution.py:39
  146.8 3.9 %collective-permute-done = bf16[8,128,128]{2,1,0:T(8,128)(2,1)S(1)} collective-permute-done((bf16[8,128,128]{2,1,0:T(8,128)(2,1)S(1)}, bf16[8,128,128]{2,1,0:T(8,128)(2,1)S(1)}, u32[]{:S(2)}, u32[]{:S(2)}) %collective-permute-start) | collective-permute-done | bytes 262176 | tf_op jit(solution)/shard_map/while/body/eval_jaxpr/ppermute | solution.py:39
  150.7 0.8 convert_element_type.83
  151.9 2.4 %fusion.53 = f32[2,8,128,128]{2,3,1,0:T(8,128)S(1)} fusion(f32[2,8,128,128]{2,3,1,0:T(8,128)} %get-tuple-element.319, f32[2,8,128,128]{2,3,1,0:T(8,128)S(1)} %copy-done.5, f32[8,128,128]{2,1,0:T(8,128)} %get-tuple-element.318), kind=kOutput, calls=%fused_computation.91 | convolution fusion | flops 402915328 | bytes 3670016 | tf_op jit(solution)/shard_map/hvk,chkl->chvl/dot_general | solution.py:145
  154.4 2.3 %multiply_reduce_fusion = (f32[2,64,8]{1,2,0:T(8,128)S(1)}, f32[2,64,8,128]{3,1,2,0:T(8,128)S(1)}) fusion(f32[2,8,64,128]{3,2,1,0:T(8,128)} %get-tuple-element.313, f32[2,8,64,128]{3,2,1,0:T(8,128)} %get-tuple-element.314, f32[2,8,128,128]{2,3,1,0:T(8,128)S(1)} %fusion.53), kind=kOutput, calls=%fused_computation.107 | convolution fusion | flops 201718784 | bytes 2625536 | tf_op jit(solution)/shard_map/chik,chvk->chiv/dot_general | solution.py:146
  158.5 0.7 copy-done.9
  159.2 1.0 fusion.61
  160.2 2.5 %collective-permute-start.3 = (bf16[128,256]{1,0:T(8,128)(2,1)}, bf16[128,256]{1,0:T(8,128)(2,1)S(1)}, u32[]{:S(2)}, u32[]{:S(2)}) collective-permute-start(bf16[128,256]{1,0:T(8,128)(2,1)} %collective-permute-done.1), channel_id=1, source_target_pairs={{0,4},{4,8},{8,12},{12,0},{1,5},{5,9},{9,13},{13,1},{2,6},{6,10},{... | collective-permute-start | bytes 196616 | tf_op jit(solution)/shard_map/ppermute | solution.py:24
  162.8 14.1 %all_gather.3 = bf16[512,256]{1,0:T(8,128)(2,1)S(1)} all-gather(bf16[128,256]{1,0:T(8,128)(2,1)S(1)} %constant_dynamic-slice_fusion.4), channel_id=1, replica_groups=mesh['groups'=2,'seq'=4,'head'=4] {'seq'}, dimensions={0}, use_global_device_ids=true | all-gather | bytes 327680 | tf_op jit(solution)/shard_map/all_gather | solution.py:175
  177.5 5.8 %conditional.1 = ((f32[4,128]{1,0:T(4,128)S(1)}, f32[4,128,256]{2,1,0:T(8,128)S(1)})) conditional(s32[]{:T(128)} %convert_element_type.52, (f32[4,128]{1,0:T(4,128)S(1)}, f32[4,128,256]{2,1,0:T(8,128)S(1)}) %tuple.53, (s32[512]{0:T(512)S(1)}, s32[512]{0:T(512)S(1)}, s32[128]{0:T(128)S(1)}, s32[128]{0:T(128)S(1)}, s32[]{:T(128)}, ...), branch_computations={%region_9.10_spmd, %region_10.13_spmd.clone.clone} | conditional | flops 270730784 | bytes 5928351 | solution.py:212
  177.5 1.3 dynamic_update_slice.50
  178.8 1.2 dynamic_update_slice.51
  180.1 1.3 dynamic_update_slice.52
  183.5 0.9 copy-done.10
  184.4 0.8 multiply_convert_fusion
  (169 shorter events, 21.2 us)
Async XLA Ops:
  0.6 0.9 copy-start
  0.7 8.7 %copy-start.11 = (bf16[128,512]{1,0:T(8,128)(2,1)S(1)}, bf16[128,512]{1,0:T(8,128)(2,1)}, u32[]{:S(2)}) copy-start(bf16[128,512]{1,0:T(8,128)(2,1)} %param.20) | copy-start | bytes 393220
  2.2 158.1 %collective-permute-start.1 = (bf16[128,256]{1,0:T(8,128)(2,1)}, bf16[128,256]{1,0:T(8,128)(2,1)}, u32[]{:S(2)}, u32[]{:S(2)}) collective-permute-start(bf16[128,256]{1,0:T(8,128)(2,1)} %constant_dynamic-slice_fusion.5), channel_id=1, source_target_pairs={{0,4},{4,8},{8,12},{12,0},{1,5},{5,9},{9,13},{13,1},{2,6},{6,10},{... | collective-permute-start | bytes 196616 | tf_op jit(solution)/shard_map/ppermute | solution.py:24
  5.2 171.6 %collective-permute-start.2 = (bf16[128,256]{1,0:T(8,128)(2,1)}, bf16[128,256]{1,0:T(8,128)(2,1)}, u32[]{:S(2)}, u32[]{:S(2)}) collective-permute-start(bf16[128,256]{1,0:T(8,128)(2,1)} %constant_dynamic-slice_fusion.5), channel_id=1, source_target_pairs={{0,12},{4,0},{8,4},{12,8},{1,13},{5,1},{9,5},{13,9},{2,14},{6,2},{... | collective-permute-start | bytes 196616 | tf_op jit(solution)/shard_map/ppermute | solution.py:29
  7.3 0.7 copy-start.22
  9.9 0.9 copy-start.12
  11.3 1.0 copy-start.8
  12.4 0.7 copy-start.19
  13.1 0.7 copy-start.18
  14.6 0.5 copy-start.25
  14.6 1.8 copy-start.13
  14.6 44.2 %copy-start.16 = (s32[2,64]{1,0:T(2,128)}, s32[2,64]{1,0:T(2,128)S(1)}, u32[]{:S(2)}) copy-start(s32[2,64]{1,0:T(2,128)S(1)} %get-tuple-element.833) | copy-start | bytes 1540 | tf_op jit(solution)/shard_map/while
  14.7 45.0 %copy-start.1 = (f32[2,8,64,128]{3,1,2,0:T(8,128)}, f32[2,8,64,128]{3,1,2,0:T(8,128)S(1)}, u32[]{:S(2)}) copy-start(f32[2,8,64,128]{3,1,2,0:T(8,128)S(1)} %get-tuple-element.837) | copy-start | bytes 1572868 | tf_op jit(solution)/shard_map/while
  62.0 1.2 copy-start.3
  62.0 1.5 copy-start.6
  63.6 2.1 %copy-start.4 = (f32[2,8,128,128]{2,3,1,0:T(8,128)}, f32[2,8,128,128]{2,3,1,0:T(8,128)S(1)}, u32[]{:S(2)}) copy-start(f32[2,8,128,128]{2,3,1,0:T(8,128)S(1)} %get-tuple-element.830) | copy-start | bytes 3145732 | tf_op jit(solution)/shard_map/while
  63.6 2.1 %copy-start.7 = (f32[2,8,128,128]{2,3,1,0:T(8,128)}, f32[2,8,128,128]{2,3,1,0:T(8,128)S(1)}, u32[]{:S(2)}) copy-start(f32[2,8,128,128]{2,3,1,0:T(8,128)S(1)} %get-tuple-element.831) | copy-start | bytes 3145732 | tf_op jit(solution)/shard_map/while
  67.5 1.1 copy-start.2
  68.6 0.7 copy-start.14
  68.6 0.7 copy-start.17
  68.6 0.7 copy-start.26
  69.3 0.5 copy-start.25
  69.3 1.8 copy-start.13
  69.3 44.2 %copy-start.16 = (s32[2,64]{1,0:T(2,128)}, s32[2,64]{1,0:T(2,128)S(1)}, u32[]{:S(2)}) copy-start(s32[2,64]{1,0:T(2,128)S(1)} %get-tuple-element.833) | copy-start | bytes 1540 | tf_op jit(solution)/shard_map/while
  69.3 45.0 %copy-start.1 = (f32[2,8,64,128]{3,1,2,0:T(8,128)}, f32[2,8,64,128]{3,1,2,0:T(8,128)S(1)}, u32[]{:S(2)}) copy-start(f32[2,8,64,128]{3,1,2,0:T(8,128)S(1)} %get-tuple-element.837) | copy-start | bytes 1572868 | tf_op jit(solution)/shard_map/while
  116.6 1.2 copy-start.3
  116.6 1.5 copy-start.6
  118.3 2.1 %copy-start.4 = (f32[2,8,128,128]{2,3,1,0:T(8,128)}, f32[2,8,128,128]{2,3,1,0:T(8,128)S(1)}, u32[]{:S(2)}) copy-start(f32[2,8,128,128]{2,3,1,0:T(8,128)S(1)} %get-tuple-element.830) | copy-start | bytes 3145732 | tf_op jit(solution)/shard_map/while
  118.3 2.1 %copy-start.7 = (f32[2,8,128,128]{2,3,1,0:T(8,128)}, f32[2,8,128,128]{2,3,1,0:T(8,128)S(1)}, u32[]{:S(2)}) copy-start(f32[2,8,128,128]{2,3,1,0:T(8,128)S(1)} %get-tuple-element.831) | copy-start | bytes 3145732 | tf_op jit(solution)/shard_map/while
  122.1 1.1 copy-start.2
  123.2 0.7 copy-start.14
  123.2 0.7 copy-start.17
  123.2 0.7 copy-start.26
  124.3 27.6 %copy-start.5 = (f32[2,8,128,128]{2,3,1,0:T(8,128)S(1)}, f32[2,8,128,128]{2,3,1,0:T(8,128)}, u32[]{:S(2)}) copy-start(f32[2,8,128,128]{2,3,1,0:T(8,128)} %get-tuple-element.315) | copy-start | bytes 3145732
  124.4 7.0 %collective-permute-start = (bf16[8,128,128]{2,1,0:T(8,128)(2,1)S(1)}, bf16[8,128,128]{2,1,0:T(8,128)(2,1)S(1)}, u32[]{:S(2)}, u32[]{:S(2)}) collective-permute-start(bf16[8,128,128]{2,1,0:T(8,128)(2,1)S(1)} %get-tuple-element.850), channel_id=1, source_target_pairs={{0,4},{4,8},{8,12},{1,5},{5,9},{9,13},{2,6},{6,10},{10,14},{3,7},{... | collective-permute-start | bytes 786440 | tf_op jit(solution)/shard_map/while/body/eval_jaxpr/ppermute | solution.py:39
  132.6 8.5 %collective-permute-start = (bf16[8,128,128]{2,1,0:T(8,128)(2,1)S(1)}, bf16[8,128,128]{2,1,0:T(8,128)(2,1)S(1)}, u32[]{:S(2)}, u32[]{:S(2)}) collective-permute-start(bf16[8,128,128]{2,1,0:T(8,128)(2,1)S(1)} %get-tuple-element.850), channel_id=1, source_target_pairs={{0,4},{4,8},{8,12},{1,5},{5,9},{9,13},{2,6},{6,10},{10,14},{3,7},{... | collective-permute-start | bytes 786440 | tf_op jit(solution)/shard_map/while/body/eval_jaxpr/ppermute | solution.py:39
  142.4 8.3 %collective-permute-start = (bf16[8,128,128]{2,1,0:T(8,128)(2,1)S(1)}, bf16[8,128,128]{2,1,0:T(8,128)(2,1)S(1)}, u32[]{:S(2)}, u32[]{:S(2)}) collective-permute-start(bf16[8,128,128]{2,1,0:T(8,128)(2,1)S(1)} %get-tuple-element.850), channel_id=1, source_target_pairs={{0,4},{4,8},{8,12},{1,5},{5,9},{9,13},{2,6},{6,10},{10,14},{3,7},{... | collective-permute-start | bytes 786440 | tf_op jit(solution)/shard_map/while/body/eval_jaxpr/ppermute | solution.py:39
  156.8 0.7 copy-start.23
  158.3 1.0 copy-start.9
  159.2 1.0 copy-start.15
  160.2 16.6 %copy-start.24 = (bf16[128,1024]{1,0:T(8,128)(2,1)S(1)}, bf16[128,1024]{1,0:T(8,128)(2,1)}, u32[]{:S(2)}) copy-start(bf16[128,1024]{1,0:T(8,128)(2,1)} %param.26) | copy-start | bytes 786436
  160.2 16.6 %collective-permute-start.3 = (bf16[128,256]{1,0:T(8,128)(2,1)}, bf16[128,256]{1,0:T(8,128)(2,1)S(1)}, u32[]{:S(2)}, u32[]{:S(2)}) collective-permute-start(bf16[128,256]{1,0:T(8,128)(2,1)} %collective-permute-done.1), channel_id=1, source_target_pairs={{0,4},{4,8},{8,12},{12,0},{1,5},{5,9},{9,13},{13,1},{2,6},{6,10},{... | collective-permute-start | bytes 196616 | tf_op jit(solution)/shard_map/ppermute | solution.py:24
  176.8 0.7 copy-start.20
  176.8 0.7 copy-start.21
  183.4 1.0 copy-start.10
